TPU v7x, 32 devices: a whole 2x2x4 slice. The times are simulated.
32 devices in a mesh: groups: 2 (over y), space: 4 (over z), chan: 2 (over x), rep: 2 (over core).
Axes of the slice: x: 2, y: 2, z: 4, core: 2. Of those that a mesh axis runs over, the one named last changes fastest.
Arguments:
- volume: bfloat16 [4, 8, 32, 8, 128], P(('groups', 'rep'), 'space', 'chan'), parts along dimension 0, may hold values from -6 to 6
- early_weight: bfloat16 [3, 3, 3, 128, 128], replicated, may hold values from -0.109375 to 0.109375
- late_weight: bfloat16 [3, 3, 3, 128, 512], P(None, None, None, None, 'chan'), may hold values from -0.109375 to 0.109375
- cotangent: bfloat16 [4, 4, 16, 4, 512], P(('groups', 'rep'), 'space', None, None, 'chan'), parts along dimension 0, may hold values from -6 to 6
Outputs:
- grad_early: bfloat16 [6, 3, 3, 128, 128], P('groups'), parts along dimension 0
- grad_late: bfloat16 [6, 3, 3, 128, 512], P('groups', None, None, None, 'chan'), parts along dimension 0
- grad_volume: bfloat16 [4, 8, 32, 8, 128], P(('groups', 'rep'), 'space', 'chan'), parts along dimension 0
There are 2 independent parts, one for each index of `groups`. A program takes and returns all parts, laid end to end along the dimension named above; an argument that names none is the same for every part. Nothing has to cross between parts.
All inputs are finite; a program needn't handle non-finite values.
Results may differ from a plain program's by a relative error of at most 0.0065.
Values may be sent and summed in bfloat16 or wider, within the bound.
No kernel may reach another device: no remote copies, remote signals or barrier semaphores. Data moves between devices by JAX's collectives and lax.ppermute only.
A program may use at most 64 MiB of HBM per device.

v0:
```python
import math
import jax
import jax.numpy as jnp
from jax import lax
from jax.sharding import PartitionSpec as P


def padded_2(block, sides, width):
    for axis, dim in sides:
        count = lax.axis_size(axis)
        forward = [(i, i + 1) for i in range(count - 1)]
        backward = [(target, source) for source, target in forward]
        low = lax.ppermute(
            lax.slice_in_dim(block, block.shape[dim] - width, None, axis=dim), axis, forward
        )
        high = lax.ppermute(lax.slice_in_dim(block, 0, width, axis=dim), axis, backward)
        block = jnp.concatenate([low, block, high], axis=dim)
    return block


def gelu_tanh(value):
    return jax.nn.gelu(value, approximate=True)


def conv_padded(padded, weight):
    depth = padded.shape[1] - 2
    height = padded.shape[2] - 2
    length = padded.shape[3] - 2
    total = None
    for first in range(3):
        for second in range(3):
            for third in range(3):
                window = padded[
                    :, first : first + depth, second : second + height, third : third + length
                ]
                term = jnp.einsum(
                    "sxyzc,co->sxyzo",
                    window,
                    weight[first, second, third],
                    preferred_element_type=jnp.float32,
                )
                total = term if total is None else total + term
    return total


def kernel_grad(padded, delta):
    depth = delta.shape[1]
    height = delta.shape[2]
    length = delta.shape[3]
    planes = []
    for first in range(3):
        for second in range(3):
            for third in range(3):
                window = padded[
                    :, first : first + depth, second : second + height, third : third + length
                ]
                planes.append(
                    jnp.einsum("sxyzc,sxyzo->co", window, delta, preferred_element_type=jnp.float32)
                )
    stacked = jnp.stack(planes, axis=0)
    return stacked.reshape((3, 3, 3) + stacked.shape[1:])


def flipped(weight):
    return jnp.swapaxes(weight[::-1, ::-1, ::-1], 3, 4)


def pad_dims(field, dims):
    widths = [(1, 1) if place in dims else (0, 0) for place in range(field.ndim)]
    return jnp.pad(field, widths)


def pool_cells(field):
    s, x, y, z, c = field.shape
    return jnp.mean(field.reshape(s, x // 2, 2, y // 2, 2, z // 2, 2, c), axis=(2, 4, 6))


def spread_cells(field):
    s, x, y, z, c = field.shape
    wide = jnp.broadcast_to(field[:, :, None, :, None, :, None, :], (s, x, 2, y, 2, z, 2, c))
    return wide.reshape(s, 2 * x, 2 * y, 2 * z, c) * 0.125


def late_layer(joined, late_weight, cotangent):
    rim = padded_2(joined, (("space", 1),), 1)
    late_pad = pad_dims(rim, (2, 3))
    pre_late = conv_padded(late_pad, late_weight)
    delta_late = jax.vjp(gelu_tanh, pre_late)[1](cotangent.astype(jnp.float32))[0].astype(
        jnp.bfloat16
    )
    late_part = kernel_grad(late_pad, delta_late)
    delta_rim = padded_2(delta_late, (("space", 1),), 1)
    back_partial = conv_padded(pad_dims(delta_rim, (2, 3)), flipped(late_weight))
    return (back_partial, late_part)


def per_device(volume, early_weight, late_weight, cotangent):
    count = (
        cotangent.shape[0]
        * lax.axis_size("rep")
        * cotangent.shape[1]
        * lax.axis_size("space")
        * cotangent.shape[2]
        * cotangent.shape[3]
    )
    scale = 1.0 / math.sqrt(count)
    haloed = padded_2(volume, (("space", 1), ("chan", 2)), 1)
    padded_in = pad_dims(haloed, (3,))
    pre_early = conv_padded(padded_in, early_weight)
    pooled = pool_cells(gelu_tanh(pre_early)).astype(jnp.bfloat16)
    joined = lax.all_gather(pooled, "chan", axis=2, tiled=True)
    back_partial, late_part = late_layer(joined, late_weight, cotangent)
    back_rows = lax.psum_scatter(back_partial, "chan", scatter_dimension=2, tiled=True)
    delta_early = jax.vjp(gelu_tanh, pre_early)[1](spread_cells(back_rows))[0].astype(jnp.bfloat16)
    early_part = kernel_grad(padded_in, delta_early)
    delta_halo = padded_2(delta_early, (("space", 1), ("chan", 2)), 1)
    grad_volume = conv_padded(pad_dims(delta_halo, (3,)), flipped(early_weight)).astype(
        jnp.bfloat16
    )
    early_total = lax.psum(early_part, ("space", "chan", "rep"))
    grad_early = (early_total * scale).astype(jnp.bfloat16)
    late_total = lax.psum(late_part, ("space", "rep"))
    grad_late = (late_total * scale).astype(jnp.bfloat16)
    return (grad_early, grad_late, grad_volume)


def solution(mesh):
    return jax.shard_map(
        per_device,
        mesh=mesh,
        in_specs=(
            P(("groups", "rep"), "space", "chan", None, None),
            P(),
            P(None, None, None, None, "chan"),
            P(("groups", "rep"), "space", None, None, "chan"),
        ),
        out_specs=(
            P("groups", None, None, None, None),
            P("groups", None, None, None, "chan"),
            P(("groups", "rep"), "space", "chan", None, None),
        ),
        check_vma=False,
    )
```

profile of v0, /device:TPU:0, one launch (start us, length us, event | category | flops | bytes accessed | tf_op | source)
XLA Modules:
  0.0 279.8 jit_solution(17251219886939649005)
XLA Ops:
  8.0 4.9 %collective-permute-start = (bf16[1,1,16,8,128]{4,3,2,1,0:T(8,128)(2,1)S(1)}, bf16[1,1,16,8,128]{4,3,2,1,0:T(8,128)(2,1)S(1)}, u32[]{:S(2)}, u32[]{:S(2)}) collective-permute-start(bf16[1,1,16,8,128]{4,3,2,1,0:T(8,128)(2,1)S(1)} %get-tuple-element.12), channel_id=1, source_target_pairs={{0,4},{4,8},{8,12},{1,5},{5,9},{9,13},{2,6},{6,10},{10,14},{3,7},{... | collective-permute-start | bytes 98312 | tf_op jit(solution)/shard_map/ppermute | solution.py:13
  12.9 1.4 collective-permute-start.1
  14.4 3.8 %copy.129 = bf16[3,3,3,128,256]{3,4,2,1,0:T(8,128)(2,1)} copy(bf16[3,3,3,128,256]{4,3,2,1,0:T(8,128)(2,1)} %param.6) | data formatting | bytes 3538944 | tf_op args[2]
  18.9 3.4 %collective-permute-start.2 = (bf16[1,4,1,8,128]{4,3,2,1,0:T(8,128)(2,1)S(1)}, bf16[1,4,1,8,128]{4,3,2,1,0:T(8,128)(2,1)S(1)}, u32[]{:S(2)}, u32[]{:S(2)}) collective-permute-start(bf16[1,4,1,8,128]{4,3,2,1,0:T(8,128)(2,1)S(1)} %get-tuple-element.7), channel_id=1, source_target_pairs={{0,2},{1,3},{4,6},{5,7},{8,10},{9,11},{12,14},{13,15},{16,18},{17,... | collective-permute-start | bytes 24584 | tf_op jit(solution)/shard_map/ppermute | solution.py:13
  22.3 1.4 collective-permute-start.3
  23.7 1.6 reverse_bitcast_fusion
  25.3 1.7 copy.133
  27.0 1.0 collective-permute-done.3
  32.5 4.5 %all-gather = bf16[16,4,128]{2,0,1:T(8,128)(2,1)S(1)} all-gather(bf16[8,4,128]{2,0,1:T(8,128)(2,1)S(1)} %fusion.279), channel_id=2, replica_groups=mesh['groups'=2,'space'=4,'chan'=2,'rep'=2] {'chan'}, dimensions={0}, use_global_device_ids=true | all-gather | bytes 24576 | tf_op jit(solution)/shard_map/all_gather | solution.py:111
  37.0 3.9 %collective-permute-start.4 = (bf16[1,1,16,4,128]{4,2,3,1,0:T(8,128)(2,1)S(1)}, bf16[1,1,16,4,128]{4,2,3,1,0:T(8,128)(2,1)S(1)}, u32[]{:S(2)}, u32[]{:S(2)}) collective-permute-start(bf16[1,1,16,4,128]{4,2,3,1,0:T(8,128)(2,1)S(1)} %bitcast.1506), channel_id=1, source_target_pairs={{0,4},{4,8},{8,12},{1,5},{5,9},{9,13},{2,6},{6,10},{10,14},{3,7},{... | collective-permute-start | bytes 49160 | tf_op jit(solution)/shard_map/ppermute | solution.py:13
  41.0 1.3 collective-permute-start.5
  42.3 1.2 reverse_bitcast_fusion.1
  43.5 3.1 %collective-permute-done.5 = bf16[1,1,16,4,128]{4,2,3,1,0:T(8,128)(2,1)S(1)} collective-permute-done((bf16[1,1,16,4,128]{4,2,3,1,0:T(8,128)(2,1)S(1)}, bf16[1,1,16,4,128]{4,2,3,1,0:T(8,128)(2,1)S(1)}, u32[]{:S(2)}, u32[]{:S(2)}) %collective-permute-start.5) | collective-permute-done | bytes 16416 | tf_op jit(solution)/shard_map/ppermute | solution.py:16
  50.5 3.5 %collective-permute-start.6 = (bf16[1,1,16,4,256]{4,2,3,1,0:T(8,128)(2,1)S(1)}, bf16[1,1,16,4,256]{4,2,3,1,0:T(8,128)(2,1)S(1)}, u32[]{:S(2)}, u32[]{:S(2)}) collective-permute-start(bf16[1,1,16,4,256]{4,2,3,1,0:T(8,128)(2,1)S(1)} %fusion.92), channel_id=1, source_target_pairs={{0,4},{4,8},{8,12},{1,5},{5,9},{9,13},{2,6},{6,10},{10,14},{3,7},{... | collective-permute-start | bytes 98312 | tf_op jit(solution)/shard_map/ppermute | solution.py:13
  54.0 1.3 collective-permute-start.7
  60.1 1.8 copy-done.1
  66.5 0.9 fusion.2
  67.3 10.6 %reduce-scatter.2.cloned.1.call-done = f32[1,1,8,4,128]{4,2,3,1,0:T(8,128)} async-done(((f32[1,1,16,4,128]{4,2,3,1,0:T(8,128)}), f32[1,1,8,4,128]{4,2,3,1,0:T(8,128)}) %reduce-scatter.2.cloned.1.call-update) | async-done | bytes 16400 | tf_op jit(solution)/shard_map/reduce_scatter | solution.py:113
  79.1 0.9 fusion.60
  85.6 1.2 copy-done.4
  87.0 3.4 %collective-permute-start.8 = (bf16[1,1,16,8,128]{4,3,2,1,0:T(8,128)(2,1)S(1)}, bf16[1,1,16,8,128]{4,3,2,1,0:T(8,128)(2,1)S(1)}, u32[]{:S(2)}, u32[]{:S(2)}) collective-permute-start(bf16[1,1,16,8,128]{4,3,2,1,0:T(8,128)(2,1)S(1)} %get-tuple-element.9), channel_id=1, source_target_pairs={{0,4},{4,8},{8,12},{1,5},{5,9},{9,13},{2,6},{6,10},{10,14},{3,7},{... | collective-permute-start | bytes 98312 | tf_op jit(solution)/shard_map/ppermute | solution.py:13
  90.4 1.3 collective-permute-start.9
  91.7 0.9 fusion.1
  92.6 3.8 %collective-permute-done.9 = bf16[1,1,16,8,128]{4,3,2,1,0:T(8,128)(2,1)S(1)} collective-permute-done((bf16[1,1,16,8,128]{4,3,2,1,0:T(8,128)(2,1)S(1)}, bf16[1,1,16,8,128]{4,3,2,1,0:T(8,128)(2,1)S(1)}, u32[]{:S(2)}, u32[]{:S(2)}) %collective-permute-start.9) | collective-permute-done | bytes 32800 | tf_op jit(solution)/shard_map/ppermute | solution.py:16
  96.4 2.7 collective-permute-start.10
  99.1 1.3 collective-permute-start.11
  100.4 0.8 fusion
  101.3 3.4 %collective-permute-done.11 = bf16[1,4,1,8,128]{4,3,2,1,0:T(8,128)(2,1)S(1)} collective-permute-done((bf16[1,4,1,8,128]{4,3,2,1,0:T(8,128)(2,1)S(1)}, bf16[1,4,1,8,128]{4,3,2,1,0:T(8,128)(2,1)S(1)}, u32[]{:S(2)}, u32[]{:S(2)}) %collective-permute-start.11) | collective-permute-done | bytes 8224 | tf_op jit(solution)/shard_map/ppermute | solution.py:16
  109.8 74.2 %all-reduce.7.cloned.1.call-done = f32[3,3,3,128,128]{4,3,2,1,0:T(8,128)} async-done(((f32[3,3,3,128,128]{4,3,2,1,0:T(8,128)}), f32[3,3,3,128,128]{4,3,2,1,0:T(8,128)}) %all-reduce.7.cloned.1.call-update) | async-done | bytes 1769488 | tf_op jit(solution)/shard_map/psum | solution.py:120
  184.0 2.6 multiply_convert_fusion.1
  186.6 83.0 %all-reduce.9.cloned.1.call-done = f32[3,3,3,128,256]{4,3,2,1,0:T(8,128)} async-done(((f32[3,3,3,128,256]{4,3,2,1,0:T(8,128)}), f32[3,3,3,128,256]{4,3,2,1,0:T(8,128)}) %all-reduce.9.cloned.1.call-update) | async-done | bytes 3538960 | tf_op jit(solution)/shard_map/psum | solution.py:122
  269.6 3.7 %multiply_convert_fusion = bf16[3,3,3,128,256]{4,3,2,1,0:T(8,128)(2,1)} fusion(f32[3,3,3,128,256]{4,3,2,1,0:T(8,128)} %all-reduce.9.cloned.1.call-done), kind=kLoop, calls=%fused_computation | loop fusion | flops 1769472 | bytes 5308416 | tf_op jit(solution)/shard_map/convert_element_type | solution.py:123
  (223 shorter events, 31.0 us)
Async XLA Ops:
  7.2 70.8 %reduce-scatter.2.cloned.1.call-start = ((), (), s32[]{:S(2)}) async-start(), calls=%async_computation.1 | async-start | bytes 49152 | tf_op jit(solution)/shard_map/reduce_scatter | solution.py:113
  8.0 10.2 %collective-permute-start = (bf16[1,1,16,8,128]{4,3,2,1,0:T(8,128)(2,1)S(1)}, bf16[1,1,16,8,128]{4,3,2,1,0:T(8,128)(2,1)S(1)}, u32[]{:S(2)}, u32[]{:S(2)}) collective-permute-start(bf16[1,1,16,8,128]{4,3,2,1,0:T(8,128)(2,1)S(1)} %get-tuple-element.12), channel_id=1, source_target_pairs={{0,4},{4,8},{8,12},{1,5},{5,9},{9,13},{2,6},{6,10},{10,14},{3,7},{... | collective-permute-start | bytes 98312 | tf_op jit(solution)/shard_map/ppermute | solution.py:13
  12.9 5.3 %copy-start.3 = (bf16[1,2,16,8,128]{4,3,2,1,0:T(8,128)(2,1)S(1)}, bf16[1,2,16,8,128]{4,3,2,1,0:T(8,128)(2,1)}, u32[]{:S(2)}) copy-start(bf16[1,2,16,8,128]{4,3,2,1,0:T(8,128)(2,1)} %param.4) | copy-start | bytes 196612
  12.9 5.9 %collective-permute-start.1 = (bf16[1,1,16,8,128]{4,3,2,1,0:T(8,128)(2,1)S(1)}, bf16[1,1,16,8,128]{4,3,2,1,0:T(8,128)(2,1)S(1)}, u32[]{:S(2)}, u32[]{:S(2)}) collective-permute-start(bf16[1,1,16,8,128]{4,3,2,1,0:T(8,128)(2,1)S(1)} %get-tuple-element.11), channel_id=1, source_target_pairs={{4,0},{8,4},{12,8},{5,1},{9,5},{13,9},{6,2},{10,6},{14,10},{7,3},{... | collective-permute-start | bytes 98312 | tf_op jit(solution)/shard_map/ppermute | solution.py:16
  18.2 11.2 %copy-start.13 = (bf16[1,1,16,8,128]{4,3,2,1,0:T(8,128)(2,1)}, bf16[1,1,16,8,128]{4,3,2,1,0:T(8,128)(2,1)S(1)}, u32[]{:S(2)}) copy-start(bf16[1,1,16,8,128]{4,3,2,1,0:T(8,128)(2,1)S(1)} %collective-permute-done) | copy-start | bytes 98308
  18.9 13.1 %copy-start.11 = (bf16[1,1,16,8,128]{4,3,2,1,0:T(8,128)(2,1)}, bf16[1,1,16,8,128]{4,3,2,1,0:T(8,128)(2,1)S(1)}, u32[]{:S(2)}) copy-start(bf16[1,1,16,8,128]{4,3,2,1,0:T(8,128)(2,1)S(1)} %collective-permute-done.1) | copy-start | bytes 98308
  18.9 8.1 %collective-permute-start.2 = (bf16[1,4,1,8,128]{4,3,2,1,0:T(8,128)(2,1)S(1)}, bf16[1,4,1,8,128]{4,3,2,1,0:T(8,128)(2,1)S(1)}, u32[]{:S(2)}, u32[]{:S(2)}) collective-permute-start(bf16[1,4,1,8,128]{4,3,2,1,0:T(8,128)(2,1)S(1)} %get-tuple-element.7), channel_id=1, source_target_pairs={{0,2},{1,3},{4,6},{5,7},{8,10},{9,11},{12,14},{13,15},{16,18},{17,... | collective-permute-start | bytes 24584 | tf_op jit(solution)/shard_map/ppermute | solution.py:13
  22.3 3.0 %copy-start.2 = (bf16[3,3,3,128,128]{4,3,2,1,0:T(8,128)(2,1)S(1)}, bf16[3,3,3,128,128]{4,3,2,1,0:T(8,128)(2,1)}, u32[]{:S(2)}) copy-start(bf16[3,3,3,128,128]{4,3,2,1,0:T(8,128)(2,1)} %param.5) | copy-start | bytes 2654212
  22.3 5.7 %collective-permute-start.3 = (bf16[1,4,1,8,128]{4,3,2,1,0:T(8,128)(2,1)S(1)}, bf16[1,4,1,8,128]{4,3,2,1,0:T(8,128)(2,1)S(1)}, u32[]{:S(2)}, u32[]{:S(2)}) collective-permute-start(bf16[1,4,1,8,128]{4,3,2,1,0:T(8,128)(2,1)S(1)} %get-tuple-element.8), channel_id=1, source_target_pairs={{2,0},{3,1},{6,4},{7,5},{10,8},{11,9},{14,12},{15,13},{18,16},{19,... | collective-permute-start | bytes 24584 | tf_op jit(solution)/shard_map/ppermute | solution.py:16
  27.0 4.6 %copy-start.9 = (bf16[1,4,1,8,128]{4,3,2,1,0:T(8,128)(2,1)}, bf16[1,4,1,8,128]{4,3,2,1,0:T(8,128)(2,1)S(1)}, u32[]{:S(2)}) copy-start(bf16[1,4,1,8,128]{4,3,2,1,0:T(8,128)(2,1)S(1)} %collective-permute-done.2) | copy-start | bytes 24580
  28.0 4.3 %copy-start.7 = (bf16[1,4,1,8,128]{4,3,2,1,0:T(8,128)(2,1)}, bf16[1,4,1,8,128]{4,3,2,1,0:T(8,128)(2,1)S(1)}, u32[]{:S(2)}) copy-start(bf16[1,4,1,8,128]{4,3,2,1,0:T(8,128)(2,1)S(1)} %collective-permute-done.3) | copy-start | bytes 24580
  32.5 14.1 %copy-start = (bf16[3,3,3,128,256]{4,3,2,1,0:T(8,128)(2,1)S(1)}, bf16[3,3,3,128,256]{4,3,2,1,0:T(8,128)(2,1)}, u32[]{:S(2)}) copy-start(bf16[3,3,3,128,256]{4,3,2,1,0:T(8,128)(2,1)} %param.6) | copy-start | bytes 5308420
  37.0 6.5 %collective-permute-start.4 = (bf16[1,1,16,4,128]{4,2,3,1,0:T(8,128)(2,1)S(1)}, bf16[1,1,16,4,128]{4,2,3,1,0:T(8,128)(2,1)S(1)}, u32[]{:S(2)}, u32[]{:S(2)}) collective-permute-start(bf16[1,1,16,4,128]{4,2,3,1,0:T(8,128)(2,1)S(1)} %bitcast.1506), channel_id=1, source_target_pairs={{0,4},{4,8},{8,12},{1,5},{5,9},{9,13},{2,6},{6,10},{10,14},{3,7},{... | collective-permute-start | bytes 49160 | tf_op jit(solution)/shard_map/ppermute | solution.py:13
  41.0 5.6 %collective-permute-start.5 = (bf16[1,1,16,4,128]{4,2,3,1,0:T(8,128)(2,1)S(1)}, bf16[1,1,16,4,128]{4,2,3,1,0:T(8,128)(2,1)S(1)}, u32[]{:S(2)}, u32[]{:S(2)}) collective-permute-start(bf16[1,1,16,4,128]{4,2,3,1,0:T(8,128)(2,1)S(1)} %bitcast.1507), channel_id=1, source_target_pairs={{4,0},{8,4},{12,8},{5,1},{9,5},{13,9},{6,2},{10,6},{14,10},{7,3},{... | collective-permute-start | bytes 49160 | tf_op jit(solution)/shard_map/ppermute | solution.py:16
  48.0 2.3 copy-start.15
  50.5 9.6 %collective-permute-start.6 = (bf16[1,1,16,4,256]{4,2,3,1,0:T(8,128)(2,1)S(1)}, bf16[1,1,16,4,256]{4,2,3,1,0:T(8,128)(2,1)S(1)}, u32[]{:S(2)}, u32[]{:S(2)}) collective-permute-start(bf16[1,1,16,4,256]{4,2,3,1,0:T(8,128)(2,1)S(1)} %fusion.92), channel_id=1, source_target_pairs={{0,4},{4,8},{8,12},{1,5},{5,9},{9,13},{2,6},{6,10},{10,14},{3,7},{... | collective-permute-start | bytes 98312 | tf_op jit(solution)/shard_map/ppermute | solution.py:13
  54.0 7.9 %collective-permute-start.7 = (bf16[1,1,16,4,256]{4,2,3,1,0:T(8,128)(2,1)S(1)}, bf16[1,1,16,4,256]{4,2,3,1,0:T(8,128)(2,1)S(1)}, u32[]{:S(2)}, u32[]{:S(2)}) collective-permute-start(bf16[1,1,16,4,256]{4,2,3,1,0:T(8,128)(2,1)S(1)} %fusion.92), channel_id=1, source_target_pairs={{4,0},{8,4},{12,8},{5,1},{9,5},{13,9},{6,2},{10,6},{14,10},{7,3},{... | collective-permute-start | bytes 98312 | tf_op jit(solution)/shard_map/ppermute | solution.py:16
  60.1 1.8 copy-start.1
  66.4 117.6 %all-reduce.7.cloned.1.call-start = ((), (), s32[]{:S(2)}) async-start(), calls=%async_computation.2 | async-start | bytes 3538944 | tf_op jit(solution)/shard_map/psum | solution.py:120
  78.8 6.6 %copy-start.5 = (bf16[2,16,8,128]{3,2,1,0:T(8,128)(2,1)}, bf16[2,16,8,128]{3,2,1,0:T(8,128)(2,1)S(1)}, u32[]{:S(2)}) copy-start(bf16[2,16,8,128]{3,2,1,0:T(8,128)(2,1)S(1)} %fusion.84) | copy-start | bytes 196612
  78.8 1.6 copy-start.14
  80.2 0.9 copy-start.8
  80.9 0.9 copy-start.10
  83.6 0.9 copy-start.12
  85.6 1.2 copy-start.4
  86.8 182.8 %all-reduce.9.cloned.1.call-start = ((), (), s32[]{:S(2)}) async-start(), calls=%async_computation.3 | async-start | bytes 7077888 | tf_op jit(solution)/shard_map/psum | solution.py:122
  87.0 5.6 %collective-permute-start.8 = (bf16[1,1,16,8,128]{4,3,2,1,0:T(8,128)(2,1)S(1)}, bf16[1,1,16,8,128]{4,3,2,1,0:T(8,128)(2,1)S(1)}, u32[]{:S(2)}, u32[]{:S(2)}) collective-permute-start(bf16[1,1,16,8,128]{4,3,2,1,0:T(8,128)(2,1)S(1)} %get-tuple-element.9), channel_id=1, source_target_pairs={{0,4},{4,8},{8,12},{1,5},{5,9},{9,13},{2,6},{6,10},{10,14},{3,7},{... | collective-permute-start | bytes 98312 | tf_op jit(solution)/shard_map/ppermute | solution.py:13
  90.4 6.0 %collective-permute-start.9 = (bf16[1,1,16,8,128]{4,3,2,1,0:T(8,128)(2,1)S(1)}, bf16[1,1,16,8,128]{4,3,2,1,0:T(8,128)(2,1)S(1)}, u32[]{:S(2)}, u32[]{:S(2)}) collective-permute-start(bf16[1,1,16,8,128]{4,3,2,1,0:T(8,128)(2,1)S(1)} %get-tuple-element.10), channel_id=1, source_target_pairs={{4,0},{8,4},{12,8},{5,1},{9,5},{13,9},{6,2},{10,6},{14,10},{7,3},{... | collective-permute-start | bytes 98312 | tf_op jit(solution)/shard_map/ppermute | solution.py:16
  96.4 4.9 %collective-permute-start.10 = (bf16[1,4,1,8,128]{4,3,2,1,0:T(8,128)(2,1)S(1)}, bf16[1,4,1,8,128]{4,3,2,1,0:T(8,128)(2,1)S(1)}, u32[]{:S(2)}, u32[]{:S(2)}) collective-permute-start(bf16[1,4,1,8,128]{4,3,2,1,0:T(8,128)(2,1)S(1)} %get-tuple-element.5), channel_id=1, source_target_pairs={{0,2},{1,3},{4,6},{5,7},{8,10},{9,11},{12,14},{13,15},{16,18},{17,... | collective-permute-start | bytes 24584 | tf_op jit(solution)/shard_map/ppermute | solution.py:13
  99.1 5.5 %collective-permute-start.11 = (bf16[1,4,1,8,128]{4,3,2,1,0:T(8,128)(2,1)S(1)}, bf16[1,4,1,8,128]{4,3,2,1,0:T(8,128)(2,1)S(1)}, u32[]{:S(2)}, u32[]{:S(2)}) collective-permute-start(bf16[1,4,1,8,128]{4,3,2,1,0:T(8,128)(2,1)S(1)} %get-tuple-element.6), channel_id=1, source_target_pairs={{2,0},{3,1},{6,4},{7,5},{10,8},{11,9},{14,12},{15,13},{18,16},{19,... | collective-permute-start | bytes 24584 | tf_op jit(solution)/shard_map/ppermute | solution.py:16
  105.5 1.4 copy-start.6
Sparse Core Ops, SparseCore 0:
  66.6 11.3 reduce-scatter.1
  87.0 96.9 all-reduce.6
  186.5 83.0 all-reduce.8
where the time goes:
time: 281 us; the launch traced here: 280 us
  waiting for transfers between devices  180 us (64%)
  matrix products  31.2 us (11%)
  starting transfers between devices  30 us (11%)
  between operations  14.4 us (5%)
  local copies, waits for them, and re-layouts  12.3 us (4%)
  other arithmetic  7.75 us (3%)
  blocking collectives  4.48 us (2%)
    psum x1, waiting for transfers between devices, per_device(): late_total = lax.psum(late_part, ('space', 'rep'))  83 us
    psum x1, waiting for transfers between devices, per_device(): early_total = lax.psum(early_part, ('space', 'chan', 'rep'))  74.2 us
    ppermute x6, starting transfers between devices, padded_2(): lax.ppermute(lax.slice_in_dim(block, block.shape[dim] - width, None, axis...  21.8 us
    dot_general x108, matrix products, conv_padded(): jnp.einsum('sxyzc,co->sxyzo', window, weight[first, second, third], prefe...  17.4 us
    dot_general x54, matrix products, kernel_grad(): jnp.einsum('sxyzc,sxyzo->co', window, delta, preferred_element_type=jnp.f...  13.9 us
    ppermute x6, waiting for transfers between devices, padded_2(): lax.ppermute(lax.slice_in_dim(block, 0, width, axis=dim), axis, backward)  11.9 us
    reduce_scatter x1, waiting for transfers between devices, per_device(): lax.psum_scatter(back_partial, 'chan', scatter_dimension=2, tiled=True)  10.6 us
    unnamed x36, local copies, waits for them, and re-layouts  8.58 us
  transfers between devices with their start and end apart: 15, of which 8 were waited for; matrix products, arithmetic and copies ran while one was open for 8% of the time, Pallas kernels for 0%

commit v1 on v0

--- a/solution.py
+++ b/solution.py
@@ -3,6 +3,12 @@
 import jax.numpy as jnp
 from jax import lax
 from jax.sharding import PartitionSpec as P
+
+
+def gather_and_add(value, mesh_axis):
+    pieces = lax.all_gather(value, mesh_axis, axis=0, tiled=False)
+    total = pieces.sum(axis=0)
+    return total
 
 
 def padded_2(block, sides, width):
@@ -117,7 +123,7 @@
     grad_volume = conv_padded(pad_dims(delta_halo, (3,)), flipped(early_weight)).astype(
         jnp.bfloat16
     )
-    early_total = lax.psum(early_part, ("space", "chan", "rep"))
+    early_total = gather_and_add(early_part, ("space", "chan", "rep"))
     grad_early = (early_total * scale).astype(jnp.bfloat16)
     late_total = lax.psum(late_part, ("space", "rep"))
     grad_late = (late_total * scale).astype(jnp.bfloat16)

time: 281 us -> 301 us (1.071)
  waiting for transfers between devices: 180 us -> 193 us
  other arithmetic: 7.75 us -> 16.5 us
  local copies, waits for them, and re-layouts: 12.3 us -> 9.06 us
    psum x1, waiting for transfers between devices: 83 us -> 169 us  [per_device(): late_total = lax.psum(late_part, ('space', 'rep'))]
    psum x1 -> x0, waiting for transfers between devices: 74.2 us -> none  [per_device(): early_total = lax.psum(early_part, ('space', 'chan', 'rep'))]
    reduce_sum x0 -> x1, other arithmetic: none -> 10.2 us  [gather_and_add(): total = pieces.sum(axis=0)]
    unnamed x36 -> x16, local copies, waits for them, and re-layouts: 8.58 us -> 8.02 us
  transfers between devices with their start and end apart: 15 -> 15, of which waited for: 8 -> 8; matrix products, arithmetic and copies ran while one was open for 8% -> 9% of each run, Pallas kernels for 0% -> 0%
where the time goes in v1:
time: 301 us; the launch traced here: 300 us
  waiting for transfers between devices  193 us (64%)
  starting transfers between devices  31.7 us (11%)
  matrix products  29.3 us (10%)
  other arithmetic  16.5 us (5%)
  between operations  16.1 us (5%)
  local copies, waits for them, and re-layouts  9.06 us (3%)
  blocking collectives  4.35 us (1%)
    psum x1, waiting for transfers between devices, per_device(): late_total = lax.psum(late_part, ('space', 'rep'))  169 us
    ppermute x6, starting transfers between devices, padded_2(): lax.ppermute(lax.slice_in_dim(block, block.shape[dim] - width, None, axis...  23.6 us
    dot_general x108, matrix products, conv_padded(): jnp.einsum('sxyzc,co->sxyzo', window, weight[first, second, third], prefe...  17.4 us
    ppermute x6, waiting for transfers between devices, padded_2(): lax.ppermute(lax.slice_in_dim(block, 0, width, axis=dim), axis, backward)  13.1 us
    dot_general x54, matrix products, kernel_grad(): jnp.einsum('sxyzc,sxyzo->co', window, delta, preferred_element_type=jnp.f...  11.9 us
    reduce_sum x1, other arithmetic, gather_and_add(): total = pieces.sum(axis=0)  10.2 us
    reduce_scatter x1, waiting for transfers between devices, per_device(): lax.psum_scatter(back_partial, 'chan', scatter_dimension=2, tiled=True)  9.39 us
    unnamed x16, local copies, waits for them, and re-layouts  8.02 us
  transfers between devices with their start and end apart: 15, of which 8 were waited for; matrix products, arithmetic and copies ran while one was open for 9% of the time, Pallas kernels for 0%

profile of v1, /device:TPU:0, one launch (start us, length us, event | category | flops | bytes accessed | tf_op | source)
XLA Modules:
  0.0 300.0 jit_solution(15391181942776073821)
XLA Ops:
  8.0 0.8 fusion.308
  8.8 4.9 %collective-permute-start = (bf16[1,1,16,8,128]{4,3,2,1,0:T(8,128)(2,1)S(1)}, bf16[1,1,16,8,128]{4,3,2,1,0:T(8,128)(2,1)S(1)}, u32[]{:S(2)}, u32[]{:S(2)}) collective-permute-start(bf16[1,1,16,8,128]{4,3,2,1,0:T(8,128)(2,1)S(1)} %get-tuple-element.12), channel_id=1, source_target_pairs={{0,4},{4,8},{8,12},{1,5},{5,9},{9,13},{2,6},{6,10},{10,14},{3,7},{... | collective-permute-start | bytes 98312 | tf_op jit(solution)/shard_map/ppermute | solution.py:19
  13.7 1.3 collective-permute-start.1
  15.3 0.9 constant_dynamic-update-slice_fusion.1
  16.2 3.4 %collective-permute-done.1 = bf16[1,1,16,8,128]{4,3,2,1,0:T(8,128)(2,1)S(1)} collective-permute-done((bf16[1,1,16,8,128]{4,3,2,1,0:T(8,128)(2,1)S(1)}, bf16[1,1,16,8,128]{4,3,2,1,0:T(8,128)(2,1)S(1)}, u32[]{:S(2)}, u32[]{:S(2)}) %collective-permute-start.1) | collective-permute-done | bytes 32800 | tf_op jit(solution)/shard_map/ppermute | solution.py:22
  19.6 3.4 %collective-permute-start.2 = (bf16[1,4,1,8,128]{4,3,2,1,0:T(8,128)(2,1)S(1)}, bf16[1,4,1,8,128]{4,3,2,1,0:T(8,128)(2,1)S(1)}, u32[]{:S(2)}, u32[]{:S(2)}) collective-permute-start(bf16[1,4,1,8,128]{4,3,2,1,0:T(8,128)(2,1)S(1)} %get-tuple-element.7), channel_id=1, source_target_pairs={{0,2},{1,3},{4,6},{5,7},{8,10},{9,11},{12,14},{13,15},{16,18},{17,... | collective-permute-start | bytes 24584 | tf_op jit(solution)/shard_map/ppermute | solution.py:19
  23.0 1.4 collective-permute-start.3
  24.4 2.8 copy.135
  27.2 1.5 collective-permute-done.3
  33.2 4.3 %all-gather = bf16[16,4,128]{2,0,1:T(8,128)(2,1)S(1)} all-gather(bf16[8,4,128]{2,0,1:T(8,128)(2,1)S(1)} %fusion.279), channel_id=2, replica_groups=mesh['groups'=2,'space'=4,'chan'=2,'rep'=2] {'chan'}, dimensions={0}, use_global_device_ids=true | all-gather | bytes 24576 | tf_op jit(solution)/shard_map/all_gather | solution.py:117
  37.6 1.4 collective-permute-start.5
  39.0 4.5 %collective-permute-start.4 = (bf16[1,1,16,4,128]{4,2,3,1,0:T(8,128)(2,1)S(1)}, bf16[1,1,16,4,128]{4,2,3,1,0:T(8,128)(2,1)S(1)}, u32[]{:S(2)}, u32[]{:S(2)}) collective-permute-start(bf16[1,1,16,4,128]{4,2,3,1,0:T(8,128)(2,1)S(1)} %bitcast.1507), channel_id=1, source_target_pairs={{0,4},{4,8},{8,12},{1,5},{5,9},{9,13},{2,6},{6,10},{10,14},{3,7},{... | collective-permute-start | bytes 49160 | tf_op jit(solution)/shard_map/ppermute | solution.py:19
  43.7 1.3 collective-permute-done.4
  48.9 1.3 collective-permute-start.7
  50.2 4.8 %collective-permute-start.6 = (bf16[1,1,16,4,256]{4,2,3,1,0:T(8,128)(2,1)S(1)}, bf16[1,1,16,4,256]{4,2,3,1,0:T(8,128)(2,1)S(1)}, u32[]{:S(2)}, u32[]{:S(2)}) collective-permute-start(bf16[1,1,16,4,256]{4,2,3,1,0:T(8,128)(2,1)S(1)} %fusion.92), channel_id=1, source_target_pairs={{0,4},{4,8},{8,12},{1,5},{5,9},{9,13},{2,6},{6,10},{10,14},{3,7},{... | collective-permute-start | bytes 98312 | tf_op jit(solution)/shard_map/ppermute | solution.py:19
  60.2 1.8 copy-done.1
  65.8 0.8 fusion.64
  66.6 0.8 fusion
  67.5 9.4 %reduce-scatter.2.cloned.1.call-done = f32[1,1,8,4,128]{4,2,3,1,0:T(8,128)} async-done(((f32[1,1,16,4,128]{4,2,3,1,0:T(8,128)}), f32[1,1,8,4,128]{4,2,3,1,0:T(8,128)}) %reduce-scatter.2.cloned.1.call-update) | async-done | bytes 16400 | tf_op jit(solution)/shard_map/reduce_scatter | solution.py:119
  83.8 1.2 copy-done.4
  85.2 3.4 %collective-permute-start.8 = (bf16[1,1,16,8,128]{4,3,2,1,0:T(8,128)(2,1)S(1)}, bf16[1,1,16,8,128]{4,3,2,1,0:T(8,128)(2,1)S(1)}, u32[]{:S(2)}, u32[]{:S(2)}) collective-permute-start(bf16[1,1,16,8,128]{4,3,2,1,0:T(8,128)(2,1)S(1)} %get-tuple-element.9), channel_id=1, source_target_pairs={{0,4},{4,8},{8,12},{1,5},{5,9},{9,13},{2,6},{6,10},{10,14},{3,7},{... | collective-permute-start | bytes 98312 | tf_op jit(solution)/shard_map/ppermute | solution.py:19
  88.6 1.3 collective-permute-start.9
  89.9 1.4 copy.139
  91.3 4.0 %collective-permute-done.9 = bf16[1,1,16,8,128]{4,3,2,1,0:T(8,128)(2,1)S(1)} collective-permute-done((bf16[1,1,16,8,128]{4,3,2,1,0:T(8,128)(2,1)S(1)}, bf16[1,1,16,8,128]{4,3,2,1,0:T(8,128)(2,1)S(1)}, u32[]{:S(2)}, u32[]{:S(2)}) %collective-permute-start.9) | collective-permute-done | bytes 32800 | tf_op jit(solution)/shard_map/ppermute | solution.py:22
  95.3 2.5 collective-permute-start.10
  97.8 1.3 collective-permute-start.11
  99.1 4.3 %collective-permute-done.11 = bf16[1,4,1,8,128]{4,3,2,1,0:T(8,128)(2,1)S(1)} collective-permute-done((bf16[1,4,1,8,128]{4,3,2,1,0:T(8,128)(2,1)S(1)}, bf16[1,4,1,8,128]{4,3,2,1,0:T(8,128)(2,1)S(1)}, u32[]{:S(2)}, u32[]{:S(2)}) %collective-permute-start.11) | collective-permute-done | bytes 8224 | tf_op jit(solution)/shard_map/ppermute | solution.py:22
  107.8 0.8 fusion.34
  108.6 168.9 %all-reduce.6.cloned.1.call-done = f32[3,3,3,128,256]{4,3,2,1,0:T(8,128)} async-done(((f32[3,3,3,128,256]{4,3,2,1,0:T(8,128)}), f32[3,3,3,128,256]{4,3,2,1,0:T(8,128)}) %all-reduce.6.cloned.1.call-update) | async-done | bytes 3538960 | tf_op jit(solution)/shard_map/psum | solution.py:128
  277.5 3.7 %multiply_convert_fusion = bf16[3,3,3,128,256]{4,3,2,1,0:T(8,128)(2,1)} fusion(f32[3,3,3,128,256]{4,3,2,1,0:T(8,128)} %all-reduce.6.cloned.1.call-done), kind=kLoop, calls=%fused_computation | loop fusion | flops 1769472 | bytes 5308416 | tf_op jit(solution)/shard_map/convert_element_type | solution.py:129
  281.2 10.2 %reduce_sum.28 = f32[3,3,3,128,128]{4,3,2,1,0:T(8,128)S(1)} reduce(f32[16,3,3,3,128,128]{5,4,3,2,1,0:T(8,128)} %all-gather.3.cloned.1.call-done, f32[]{:T(128)} %constant.5.clone.1), dimensions={0}, to_apply=%region_3.4 | reduce | flops 6635520 | bytes 30081028 | tf_op jit(solution)/shard_map/reduce_sum | solution.py:10
  291.4 1.2 multiply_convert_fusion.1
  (204 shorter events, 29.1 us)
Async XLA Ops:
  8.0 68.9 %reduce-scatter.2.cloned.1.call-start = ((), (), s32[]{:S(2)}) async-start(), calls=%async_computation.1 | async-start | bytes 49152 | tf_op jit(solution)/shard_map/reduce_scatter | solution.py:119
  8.8 6.5 %collective-permute-start = (bf16[1,1,16,8,128]{4,3,2,1,0:T(8,128)(2,1)S(1)}, bf16[1,1,16,8,128]{4,3,2,1,0:T(8,128)(2,1)S(1)}, u32[]{:S(2)}, u32[]{:S(2)}) collective-permute-start(bf16[1,1,16,8,128]{4,3,2,1,0:T(8,128)(2,1)S(1)} %get-tuple-element.12), channel_id=1, source_target_pairs={{0,4},{4,8},{8,12},{1,5},{5,9},{9,13},{2,6},{6,10},{10,14},{3,7},{... | collective-permute-start | bytes 98312 | tf_op jit(solution)/shard_map/ppermute | solution.py:19
  13.7 5.8 %collective-permute-start.1 = (bf16[1,1,16,8,128]{4,3,2,1,0:T(8,128)(2,1)S(1)}, bf16[1,1,16,8,128]{4,3,2,1,0:T(8,128)(2,1)S(1)}, u32[]{:S(2)}, u32[]{:S(2)}) collective-permute-start(bf16[1,1,16,8,128]{4,3,2,1,0:T(8,128)(2,1)S(1)} %get-tuple-element.11), channel_id=1, source_target_pairs={{4,0},{8,4},{12,8},{5,1},{9,5},{13,9},{6,2},{10,6},{14,10},{7,3},{... | collective-permute-start | bytes 98312 | tf_op jit(solution)/shard_map/ppermute | solution.py:22
  19.6 7.6 %collective-permute-start.2 = (bf16[1,4,1,8,128]{4,3,2,1,0:T(8,128)(2,1)S(1)}, bf16[1,4,1,8,128]{4,3,2,1,0:T(8,128)(2,1)S(1)}, u32[]{:S(2)}, u32[]{:S(2)}) collective-permute-start(bf16[1,4,1,8,128]{4,3,2,1,0:T(8,128)(2,1)S(1)} %get-tuple-element.7), channel_id=1, source_target_pairs={{0,2},{1,3},{4,6},{5,7},{8,10},{9,11},{12,14},{13,15},{16,18},{17,... | collective-permute-start | bytes 24584 | tf_op jit(solution)/shard_map/ppermute | solution.py:19
  23.0 5.8 %copy-start.2 = (bf16[3,3,3,128,128]{4,3,2,1,0:T(8,128)(2,1)S(1)}, bf16[3,3,3,128,128]{4,3,2,1,0:T(8,128)(2,1)}, u32[]{:S(2)}) copy-start(bf16[3,3,3,128,128]{4,3,2,1,0:T(8,128)(2,1)} %param.5) | copy-start | bytes 2654212
  23.0 5.7 %collective-permute-start.3 = (bf16[1,4,1,8,128]{4,3,2,1,0:T(8,128)(2,1)S(1)}, bf16[1,4,1,8,128]{4,3,2,1,0:T(8,128)(2,1)S(1)}, u32[]{:S(2)}, u32[]{:S(2)}) collective-permute-start(bf16[1,4,1,8,128]{4,3,2,1,0:T(8,128)(2,1)S(1)} %get-tuple-element.8), channel_id=1, source_target_pairs={{2,0},{3,1},{6,4},{7,5},{10,8},{11,9},{14,12},{15,13},{18,16},{19,... | collective-permute-start | bytes 24584 | tf_op jit(solution)/shard_map/ppermute | solution.py:22
  27.2 2.9 copy-start.3
  37.6 7.4 %copy-start = (bf16[3,3,3,128,256]{4,3,2,1,0:T(8,128)(2,1)S(1)}, bf16[3,3,3,128,256]{4,3,2,1,0:T(8,128)(2,1)}, u32[]{:S(2)}) copy-start(bf16[3,3,3,128,256]{4,3,2,1,0:T(8,128)(2,1)} %param.6) | copy-start | bytes 5308420
  37.6 6.1 %collective-permute-start.5 = (bf16[1,1,16,4,128]{4,2,3,1,0:T(8,128)(2,1)S(1)}, bf16[1,1,16,4,128]{4,2,3,1,0:T(8,128)(2,1)S(1)}, u32[]{:S(2)}, u32[]{:S(2)}) collective-permute-start(bf16[1,1,16,4,128]{4,2,3,1,0:T(8,128)(2,1)S(1)} %bitcast.1506), channel_id=1, source_target_pairs={{4,0},{8,4},{12,8},{5,1},{9,5},{13,9},{6,2},{10,6},{14,10},{7,3},{... | collective-permute-start | bytes 49160 | tf_op jit(solution)/shard_map/ppermute | solution.py:22
  39.0 6.0 %collective-permute-start.4 = (bf16[1,1,16,4,128]{4,2,3,1,0:T(8,128)(2,1)S(1)}, bf16[1,1,16,4,128]{4,2,3,1,0:T(8,128)(2,1)S(1)}, u32[]{:S(2)}, u32[]{:S(2)}) collective-permute-start(bf16[1,1,16,4,128]{4,2,3,1,0:T(8,128)(2,1)S(1)} %bitcast.1507), channel_id=1, source_target_pairs={{0,4},{4,8},{8,12},{1,5},{5,9},{9,13},{2,6},{6,10},{10,14},{3,7},{... | collective-permute-start | bytes 49160 | tf_op jit(solution)/shard_map/ppermute | solution.py:19
  46.4 2.3 copy-start.5
  48.9 11.4 %collective-permute-start.7 = (bf16[1,1,16,4,256]{4,2,3,1,0:T(8,128)(2,1)S(1)}, bf16[1,1,16,4,256]{4,2,3,1,0:T(8,128)(2,1)S(1)}, u32[]{:S(2)}, u32[]{:S(2)}) collective-permute-start(bf16[1,1,16,4,256]{4,2,3,1,0:T(8,128)(2,1)S(1)} %fusion.92), channel_id=1, source_target_pairs={{4,0},{8,4},{12,8},{5,1},{9,5},{13,9},{6,2},{10,6},{14,10},{7,3},{... | collective-permute-start | bytes 98312 | tf_op jit(solution)/shard_map/ppermute | solution.py:22
  50.2 11.9 %collective-permute-start.6 = (bf16[1,1,16,4,256]{4,2,3,1,0:T(8,128)(2,1)S(1)}, bf16[1,1,16,4,256]{4,2,3,1,0:T(8,128)(2,1)S(1)}, u32[]{:S(2)}, u32[]{:S(2)}) collective-permute-start(bf16[1,1,16,4,256]{4,2,3,1,0:T(8,128)(2,1)S(1)} %fusion.92), channel_id=1, source_target_pairs={{0,4},{4,8},{8,12},{1,5},{5,9},{9,13},{2,6},{6,10},{10,14},{3,7},{... | collective-permute-start | bytes 98312 | tf_op jit(solution)/shard_map/ppermute | solution.py:19
  60.2 1.8 copy-start.1
  66.5 210.9 %all-reduce.6.cloned.1.call-start = ((), (), s32[]{:S(2)}) async-start(), calls=%async_computation.3 | async-start | bytes 7077888 | tf_op jit(solution)/shard_map/psum | solution.py:128
  67.5 213.7 %all-gather.3.cloned.1.call-start = ((), (), s32[]{:S(2)}) async-start(), calls=%async_computation.2 | async-start | bytes 30081024 | tf_op jit(solution)/shard_map/all_gather | solution.py:9
  83.8 1.2 copy-start.4
  85.2 6.1 %collective-permute-start.8 = (bf16[1,1,16,8,128]{4,3,2,1,0:T(8,128)(2,1)S(1)}, bf16[1,1,16,8,128]{4,3,2,1,0:T(8,128)(2,1)S(1)}, u32[]{:S(2)}, u32[]{:S(2)}) collective-permute-start(bf16[1,1,16,8,128]{4,3,2,1,0:T(8,128)(2,1)S(1)} %get-tuple-element.9), channel_id=1, source_target_pairs={{0,4},{4,8},{8,12},{1,5},{5,9},{9,13},{2,6},{6,10},{10,14},{3,7},{... | collective-permute-start | bytes 98312 | tf_op jit(solution)/shard_map/ppermute | solution.py:19
  88.6 6.7 %collective-permute-start.9 = (bf16[1,1,16,8,128]{4,3,2,1,0:T(8,128)(2,1)S(1)}, bf16[1,1,16,8,128]{4,3,2,1,0:T(8,128)(2,1)S(1)}, u32[]{:S(2)}, u32[]{:S(2)}) collective-permute-start(bf16[1,1,16,8,128]{4,3,2,1,0:T(8,128)(2,1)S(1)} %get-tuple-element.10), channel_id=1, source_target_pairs={{4,0},{8,4},{12,8},{5,1},{9,5},{13,9},{6,2},{10,6},{14,10},{7,3},{... | collective-permute-start | bytes 98312 | tf_op jit(solution)/shard_map/ppermute | solution.py:22
  95.3 3.9 %collective-permute-start.10 = (bf16[1,4,1,8,128]{4,3,2,1,0:T(8,128)(2,1)S(1)}, bf16[1,4,1,8,128]{4,3,2,1,0:T(8,128)(2,1)S(1)}, u32[]{:S(2)}, u32[]{:S(2)}) collective-permute-start(bf16[1,4,1,8,128]{4,3,2,1,0:T(8,128)(2,1)S(1)} %get-tuple-element.5), channel_id=1, source_target_pairs={{0,2},{1,3},{4,6},{5,7},{8,10},{9,11},{12,14},{13,15},{16,18},{17,... | collective-permute-start | bytes 24584 | tf_op jit(solution)/shard_map/ppermute | solution.py:19
  97.8 5.7 %collective-permute-start.11 = (bf16[1,4,1,8,128]{4,3,2,1,0:T(8,128)(2,1)S(1)}, bf16[1,4,1,8,128]{4,3,2,1,0:T(8,128)(2,1)S(1)}, u32[]{:S(2)}, u32[]{:S(2)}) collective-permute-start(bf16[1,4,1,8,128]{4,3,2,1,0:T(8,128)(2,1)S(1)} %get-tuple-element.6), channel_id=1, source_target_pairs={{2,0},{3,1},{6,4},{7,5},{10,8},{11,9},{14,12},{15,13},{18,16},{19,... | collective-permute-start | bytes 24584 | tf_op jit(solution)/shard_map/ppermute | solution.py:22
Sparse Core Ops, SparseCore 0:
  66.7 10.1 reduce-scatter.1
  85.2 170.5 all-gather.2
Sparse Core Ops, SparseCore 1:
  69.4 208.0 all-reduce.5
